TPU v7x, 32 devices: a whole 2x2x4 slice. The times are simulated.
32 devices in a mesh: row: 4 (over x, core), col: 8 (over z, y).
Axes of the slice: x: 2, y: 2, z: 4, core: 2. Of those that a mesh axis runs over, the one named last changes fastest.
Arguments:
- item_ids: int32 [8192], P(('row', 'col')), may hold values from 0 to 63
- user_lengths: int32 [8], replicated, may hold values from 1 to 2048, 8192 in all
- catalogue: bfloat16 [64, 1024], P(('row', 'col')), may hold values from -6 to 6
- tap_lengths: int32 [1, 1024], replicated, may hold values from 64 to 256
- conv_taps: bfloat16 [1, 256, 1024], replicated, may hold values from -0.375 to 0.375
- norm_gains: float32 [1, 2, 1024], replicated, may hold values from 0.1 to 1.9
- gate_weight: bfloat16 [1, 1024, 1024], P(None, 'col'), may hold values from -0.1875 to 0.1875
- up_weight: bfloat16 [1, 1024, 1024], P(None, 'col'), may hold values from -0.1875 to 0.1875
- down_weight: bfloat16 [1, 1024, 1024], P(None, 'col'), may hold values from -0.1875 to 0.1875
Outputs:
- history_out: bfloat16 [8192, 1024], P(('row', 'col'))
Inputs may be any that keep to these rules, and one draw needn't show every extreme that they name: `user_lengths`: the 8 lengths sum to 8192.
All inputs are finite; a program needn't handle non-finite values.
Results may differ from a plain program's by a relative error of at most 0.0054.
Values may be sent and summed in bfloat16 or wider, within the bound.
No kernel may reach another device: no remote copies, remote signals or barrier semaphores. Data moves between devices by JAX's collectives and lax.ppermute only.
A program may use at most 64 MiB of HBM per device.

v0:
```python
import jax
import jax.numpy as jnp
from jax import lax
from jax.sharding import PartitionSpec as P

epsilon = 1e-06
group_taps = 32


def from_behind(block, axis, distance):
    devices = range(lax.axis_size(axis))
    route = [(i - distance, i) for i in devices if i - distance in devices]
    return lax.ppermute(block, axis, route)


def rms_norm(values, gains):
    scale = lax.rsqrt(jnp.mean(values * values, axis=-1, keepdims=True) + epsilon)
    return values * scale * gains


def token_ages(positions, user_starts):
    reached = user_starts[None, :] <= positions[:, None]
    fallback = jnp.minimum(positions, 0)[:, None]
    seg_start = jnp.max(jnp.where(reached, user_starts[None, :], fallback), axis=1)
    return positions - seg_start


def earlier_items(item_ids, wanted):
    current = item_ids
    pieces = []
    current = from_behind(current, ("row", "col"), 1)
    pieces = [current] + pieces
    return pieces[0][-wanted:]


def convolve(extended, tap_table, token_age, out_rows):
    reach = extended.shape[0] - out_rows
    groups = -(-tap_table.shape[0] // group_taps)

    def one_group(group_index, accumulated):
        for within in range(group_taps):
            lag_index = group_index * group_taps + within
            shifted = lax.dynamic_slice_in_dim(extended, reach - lag_index, out_rows, 0)
            weights = lax.dynamic_slice_in_dim(tap_table, lag_index, 1, 0)
            keep = (lag_index <= token_age)[:, None]
            accumulated = accumulated + jnp.where(keep, shifted * weights, 0.0)
        return accumulated

    blank = jnp.zeros((out_rows, extended.shape[1]), jnp.float32)
    return lax.fori_loop(0, groups, one_group, blank)


def feed_forward(hidden, gains_row, gate_rows, up_rows, down_rows):
    inner = rms_norm(hidden, gains_row).astype(jnp.bfloat16)
    columns = inner
    first_sum = jnp.dot(
        columns,
        lax.all_gather(gate_rows, "col", axis=0, tiled=True),
        preferred_element_type=jnp.float32,
    )
    second_sum = jnp.dot(
        columns,
        lax.all_gather(up_rows, "col", axis=0, tiled=True),
        preferred_element_type=jnp.float32,
    )
    activated = (jax.nn.silu(first_sum) * second_sum).astype(jnp.bfloat16)
    columns = activated
    projected = jnp.dot(
        columns,
        lax.all_gather(down_rows, "col", axis=0, tiled=True),
        preferred_element_type=jnp.float32,
    )
    return hidden + projected


def body(
    item_ids,
    user_lengths,
    catalogue,
    tap_lengths,
    conv_taps,
    norm_gains,
    gate_weight,
    up_weight,
    down_weight,
):
    row_count = item_ids.shape[0]
    reach = conv_taps.shape[1] - 1
    layer_count = conv_taps.shape[0]
    catalogue_all = lax.all_gather(catalogue, ("row", "col"), axis=0, tiled=True)
    device_index = lax.axis_index("row") * lax.axis_size("col") + lax.axis_index("col")
    first_row = device_index * row_count
    user_starts = jnp.cumsum(user_lengths) - user_lengths
    lag_column = jnp.arange(conv_taps.shape[1], dtype=jnp.int32)[:, None]
    tap_tables = conv_taps.astype(jnp.float32) * (
        lag_column[None] < tap_lengths[:, None, :]
    ).astype(jnp.float32)
    extra = reach * layer_count
    wide_ids = jnp.concatenate([earlier_items(item_ids, extra), item_ids], axis=0)
    hidden = jnp.take(catalogue_all, wide_ids, axis=0).astype(jnp.float32)
    positions = first_row - extra + jnp.arange(row_count + extra, dtype=jnp.int32)
    all_ages = token_ages(positions, user_starts)
    out_rows = row_count + reach * (layer_count - 1)
    normed = rms_norm(hidden, norm_gains[0, 0]).astype(jnp.bfloat16)
    hidden = hidden[-out_rows:] + convolve(normed, tap_tables[0], all_ages[-out_rows:], out_rows)
    hidden = feed_forward(hidden, norm_gains[0, 1], gate_weight[0], up_weight[0], down_weight[0])
    return hidden.astype(jnp.bfloat16)


def solution(mesh):
    return jax.shard_map(
        body,
        mesh=mesh,
        in_specs=(
            P(("row", "col")),
            P(),
            P(("row", "col"), None),
            P(),
            P(),
            P(),
            P(None, "col", None),
            P(None, "col", None),
            P(None, "col", None),
        ),
        out_specs=P(("row", "col"), None),
        check_vma=False,
    )
```

profile of v0, /device:TPU:2, one launch (start us, length us, event | category | flops | bytes accessed | tf_op | source)
XLA Modules:
  0.0 230.7 jit_solution(10582264455192001664)
XLA Ops:
  8.1 3.4 %collective-permute-start = (s32[256]{0:T(256)}, s32[256]{0:T(256)S(1)}, u32[]{:S(2)}, u32[]{:S(2)}) collective-permute-start(s32[256]{0:T(256)} %param.11), channel_id=1, source_target_pairs={{0,1},{1,2},{2,3},{3,4},{4,5},{5,6},{6,7},{7,8},{8,9},{9,10},{10,1... | collective-permute-start | bytes 3080 | tf_op jit(solution)/shard_map/ppermute | solution.py:13
  13.9 2.2 select_bitcast_fusion
  16.1 69.4 %all-gather.3 = bf16[32,2,1024]{2,1,0:T(2,128)(2,1)S(1)} all-gather(bf16[1,2,1024]{2,1,0:T(2,128)(2,1)S(1)} %bitcast.163), channel_id=1, replica_groups=mesh['row'=4,'col'=8] {'row','col'}, dimensions={0}, use_global_device_ids=true | all-gather | bytes 135168 | tf_op jit(solution)/shard_map/all_gather | solution.py:90
  85.9 2.1 gather_fusion
  88.8 124.7 %while.17 = (s32[]{:T(128)}, f32[256,1024]{1,0:T(8,128)S(1)}, s32[256]{0:T(256)S(1)}, bf16[511,1024]{1,0:T(8,128)(2,1)S(1)}, f32[256,1024]{1,0:T(8,128)}, /*inde...) while((s32[]{:T(128)}, f32[256,1024]{1,0:T(8,128)S(1)}, ...), condition=%wide.region_4.5_spmd.clone, body=%wide.region_3.4_spmd.clone.sunk | while | flops 33825024 | bytes 19289948 | solution.py:50
  88.9 1.5 constant_dynamic-slice_fusion.35
  90.5 1.4 constant_dynamic-slice_fusion.34
  92.3 12.3 %select_add_fusion.3 = f32[256,1024]{1,0:T(8,128)S(1)} fusion(f32[256,1024]{1,0:T(8,128)S(1)} %get-tuple-element.605, f32[1024]{0:T(1024)S(1)} %bitcast.128, bf16[511,1024]{1,0:T(8,128)(2,1)S(1)} %get-tuple-element.679, s32[]{:T(128)S(6)} %select_n.1373, f32[1024]{0:T(1024)S(1)} %bitcast.129, s32[]{:T(128)S(6)} %select_n.1374, ...), kind=kLoop, calls=%fused_computation.26.clone.1 | loop fusion | flops 33816576 | bytes 19013760 | tf_op jit(solution)/shard_map/while/body/eval_jaxpr/add | solution.py:46
  104.7 1.2 constant_dynamic-slice_fusion.35
  106.1 1.4 constant_dynamic-slice_fusion.34
  107.8 12.3 %select_add_fusion.3 = f32[256,1024]{1,0:T(8,128)S(1)} fusion(f32[256,1024]{1,0:T(8,128)S(1)} %get-tuple-element.605, f32[1024]{0:T(1024)S(1)} %bitcast.128, bf16[511,1024]{1,0:T(8,128)(2,1)S(1)} %get-tuple-element.679, s32[]{:T(128)S(6)} %select_n.1373, f32[1024]{0:T(1024)S(1)} %bitcast.129, s32[]{:T(128)S(6)} %select_n.1374, ...), kind=kLoop, calls=%fused_computation.26.clone.1 | loop fusion | flops 33816576 | bytes 19013760 | tf_op jit(solution)/shard_map/while/body/eval_jaxpr/add | solution.py:46
  120.3 1.2 constant_dynamic-slice_fusion.35
  121.6 1.4 constant_dynamic-slice_fusion.34
  123.4 12.3 %select_add_fusion.3 = f32[256,1024]{1,0:T(8,128)S(1)} fusion(f32[256,1024]{1,0:T(8,128)S(1)} %get-tuple-element.605, f32[1024]{0:T(1024)S(1)} %bitcast.128, bf16[511,1024]{1,0:T(8,128)(2,1)S(1)} %get-tuple-element.679, s32[]{:T(128)S(6)} %select_n.1373, f32[1024]{0:T(1024)S(1)} %bitcast.129, s32[]{:T(128)S(6)} %select_n.1374, ...), kind=kLoop, calls=%fused_computation.26.clone.1 | loop fusion | flops 33816576 | bytes 19013760 | tf_op jit(solution)/shard_map/while/body/eval_jaxpr/add | solution.py:46
  135.8 1.2 constant_dynamic-slice_fusion.35
  137.2 1.4 constant_dynamic-slice_fusion.34
  138.9 12.3 %select_add_fusion.3 = f32[256,1024]{1,0:T(8,128)S(1)} fusion(f32[256,1024]{1,0:T(8,128)S(1)} %get-tuple-element.605, f32[1024]{0:T(1024)S(1)} %bitcast.128, bf16[511,1024]{1,0:T(8,128)(2,1)S(1)} %get-tuple-element.679, s32[]{:T(128)S(6)} %select_n.1373, f32[1024]{0:T(1024)S(1)} %bitcast.129, s32[]{:T(128)S(6)} %select_n.1374, ...), kind=kLoop, calls=%fused_computation.26.clone.1 | loop fusion | flops 33816576 | bytes 19013760 | tf_op jit(solution)/shard_map/while/body/eval_jaxpr/add | solution.py:46
  151.4 1.2 constant_dynamic-slice_fusion.35
  152.7 1.4 constant_dynamic-slice_fusion.34
  154.5 12.3 %select_add_fusion.3 = f32[256,1024]{1,0:T(8,128)S(1)} fusion(f32[256,1024]{1,0:T(8,128)S(1)} %get-tuple-element.605, f32[1024]{0:T(1024)S(1)} %bitcast.128, bf16[511,1024]{1,0:T(8,128)(2,1)S(1)} %get-tuple-element.679, s32[]{:T(128)S(6)} %select_n.1373, f32[1024]{0:T(1024)S(1)} %bitcast.129, s32[]{:T(128)S(6)} %select_n.1374, ...), kind=kLoop, calls=%fused_computation.26.clone.1 | loop fusion | flops 33816576 | bytes 19013760 | tf_op jit(solution)/shard_map/while/body/eval_jaxpr/add | solution.py:46
  166.9 1.2 constant_dynamic-slice_fusion.35
  168.3 1.4 constant_dynamic-slice_fusion.34
  170.0 12.3 %select_add_fusion.3 = f32[256,1024]{1,0:T(8,128)S(1)} fusion(f32[256,1024]{1,0:T(8,128)S(1)} %get-tuple-element.605, f32[1024]{0:T(1024)S(1)} %bitcast.128, bf16[511,1024]{1,0:T(8,128)(2,1)S(1)} %get-tuple-element.679, s32[]{:T(128)S(6)} %select_n.1373, f32[1024]{0:T(1024)S(1)} %bitcast.129, s32[]{:T(128)S(6)} %select_n.1374, ...), kind=kLoop, calls=%fused_computation.26.clone.1 | loop fusion | flops 33816576 | bytes 19013760 | tf_op jit(solution)/shard_map/while/body/eval_jaxpr/add | solution.py:46
  182.5 1.2 constant_dynamic-slice_fusion.35
  183.8 1.4 constant_dynamic-slice_fusion.34
  185.6 12.3 %select_add_fusion.3 = f32[256,1024]{1,0:T(8,128)S(1)} fusion(f32[256,1024]{1,0:T(8,128)S(1)} %get-tuple-element.605, f32[1024]{0:T(1024)S(1)} %bitcast.128, bf16[511,1024]{1,0:T(8,128)(2,1)S(1)} %get-tuple-element.679, s32[]{:T(128)S(6)} %select_n.1373, f32[1024]{0:T(1024)S(1)} %bitcast.129, s32[]{:T(128)S(6)} %select_n.1374, ...), kind=kLoop, calls=%fused_computation.26.clone.1 | loop fusion | flops 33816576 | bytes 19013760 | tf_op jit(solution)/shard_map/while/body/eval_jaxpr/add | solution.py:46
  198.0 1.2 constant_dynamic-slice_fusion.35
  199.4 1.4 constant_dynamic-slice_fusion.34
  201.2 12.3 %select_add_fusion.3 = f32[256,1024]{1,0:T(8,128)S(1)} fusion(f32[256,1024]{1,0:T(8,128)S(1)} %get-tuple-element.605, f32[1024]{0:T(1024)S(1)} %bitcast.128, bf16[511,1024]{1,0:T(8,128)(2,1)S(1)} %get-tuple-element.679, s32[]{:T(128)S(6)} %select_n.1373, f32[1024]{0:T(1024)S(1)} %bitcast.129, s32[]{:T(128)S(6)} %select_n.1374, ...), kind=kLoop, calls=%fused_computation.26.clone.1 | loop fusion | flops 33816576 | bytes 19013760 | tf_op jit(solution)/shard_map/while/body/eval_jaxpr/add | solution.py:46
  213.7 1.3 copy-done
  215.4 3.9 %fusion.28 = f32[256,1024]{1,0:T(8,128)} fusion(bf16[1,1024,1024]{2,1,0:T(8,128)(2,1)} %all-gather.8.cloned.1.call-done, f32[1024]{0:T(1024)S(1)} %bitcast.165, f32[256]{0:T(256)S(1)} %add_rsqrt_fusion.1, f32[256,1024]{1,0:T(8,128)S(1)} %get-tuple-element.276, f32[511,1024]{1,0:T(8,128)} %copy-done), kind=kOutput, calls=%fused_computation.95 | convolution fusion | flops 537919488 | bytes 5248000 | tf_op jit(solution)/shard_map/dot_general | solution.py:56
  219.3 4.9 %fusion.36 = bf16[256,1024]{1,0:T(8,128)(2,1)} fusion(bf16[1,1024,1024]{2,1,0:T(8,128)(2,1)} %all-gather.12.cloned.1.call-done, bf16[1,1024,1024]{2,1,0:T(8,128)(2,1)} %all-gather.10.cloned.1.call-done, f32[256,1024]{1,0:T(8,128)} %fusion.28, f32[1024]{0:T(1024)S(1)} %bitcast.166, f32[256]{0:T(256)S(1)} %add_rsqrt_fusion.1, ...), kind=kOutput, calls=%fused_computation.101 | convolution fusion | flops 1077149696 | bytes 9966592 | tf_op jit(solution)/shard_map/dot_general | solution.py:68
  (52 shorter events, 6.1 us)
Async XLA Ops:
  6.5 79.2 %copy-start.3 = (s32[256]{0:T(256)S(1)}, s32[256]{0:T(256)}, u32[]{:S(2)}) copy-start(s32[256]{0:T(256)} %param.11) | copy-start | bytes 3076
  6.5 9.6 %copy-start.2 = (bf16[2,1024]{1,0:T(2,128)(2,1)S(1)}, bf16[2,1024]{1,0:T(2,128)(2,1)}, u32[]{:S(2)}) copy-start(bf16[2,1024]{1,0:T(2,128)(2,1)} %param.13) | copy-start | bytes 12292
  6.5 208.8 %all-gather.8.cloned.1.call-start = ((), (), s32[]{:S(2)}) async-start(), calls=%async_computation | async-start | bytes 2359296 | tf_op jit(solution)/shard_map/all_gather | solution.py:58
  7.3 212.0 %all-gather.10.cloned.1.call-start = ((), (), s32[]{:S(2)}) async-start(), calls=%async_computation.1 | async-start | bytes 2359296 | tf_op jit(solution)/shard_map/all_gather | solution.py:63
  8.0 211.3 %all-gather.12.cloned.1.call-start = ((), (), s32[]{:S(2)}) async-start(), calls=%async_computation.2 | async-start | bytes 2359296 | tf_op jit(solution)/shard_map/all_gather | solution.py:70
  8.1 77.6 %collective-permute-start = (s32[256]{0:T(256)}, s32[256]{0:T(256)S(1)}, u32[]{:S(2)}, u32[]{:S(2)}) collective-permute-start(s32[256]{0:T(256)} %param.11), channel_id=1, source_target_pairs={{0,1},{1,2},{2,3},{3,4},{4,5},{5,6},{6,7},{7,8},{8,9},{9,10},{10,1... | collective-permute-start | bytes 3080 | tf_op jit(solution)/shard_map/ppermute | solution.py:13
  213.7 1.4 copy-start
  215.4 3.9 %copy-start.1 = (f32[511,1024]{1,0:T(8,128)S(1)}, f32[511,1024]{1,0:T(8,128)}, u32[]{:S(2)}) copy-start(f32[511,1024]{1,0:T(8,128)} %copy-done) | copy-start | bytes 6279172
Sparse Core Ops, SparseCore 0:
  9.5 50.3 all-gather.7
  62.0 48.4 all-gather.9
  112.6 47.6 all-gather.11
where the time goes:
time: 233 us; the launch traced here: 231 us
  other arithmetic  104 us (45%)
  blocking collectives  69.4 us (30%)
  local copies, waits for them, and re-layouts  25.8 us (11%)
  between operations  13.2 us (6%)
  matrix products  8.77 us (4%)
  loops' own time  4.23 us (2%)
  starting transfers between devices  3.51 us (2%)
    add x8, other arithmetic, one_group(): accumulated = accumulated + jnp.where(keep, shifted * weights, 0.0)  98.5 us
    all_gather x1, blocking collectives, body(): lax.all_gather(catalogue, ('row', 'col'), axis=0, tiled=True)  69.4 us
    dynamic_slice x16, local copies, waits for them, and re-layouts, one_group(): weights = lax.dynamic_slice_in_dim(tap_table, lag_index, 1, 0)  21.4 us
    dot_general x1, matrix products, feed_forward(): jnp.dot(columns, lax.all_gather(down_rows, 'col', axis=0, tiled=True), pr...  4.87 us
  transfers between devices with their start and end apart: 4, of which 0 were waited for; matrix products, arithmetic and copies ran while one was open for 57% of the time, Pallas kernels for 0%

commit v1 on v0

--- a/solution.py
+++ b/solution.py
@@ -87,7 +87,15 @@
     row_count = item_ids.shape[0]
     reach = conv_taps.shape[1] - 1
     layer_count = conv_taps.shape[0]
-    catalogue_all = lax.all_gather(catalogue, ("row", "col"), axis=0, tiled=True)
+    catalogue_all = jnp.concatenate(
+        lax.all_to_all(
+            jnp.stack([catalogue] * lax.axis_size(("row", "col"))),
+            axis_name=("row", "col"),
+            split_axis=0,
+            concat_axis=0,
+        ),
+        axis=0,
+    )
     device_index = lax.axis_index("row") * lax.axis_size("col") + lax.axis_index("col")
     first_row = device_index * row_count
     user_starts = jnp.cumsum(user_lengths) - user_lengths

time: 233 us -> 177 us (0.76)
  the two profiles are of different devices: /device:TPU:2 before, /device:TPU:0 now
where the time goes in v1:
time: 177 us; the launch traced here: 175 us
  other arithmetic  104 us (59%)
  local copies, waits for them, and re-layouts  29.5 us (17%)
  between operations  13.2 us (7%)
  starting transfers between devices  9.88 us (6%)
  matrix products  8.79 us (5%)
  waiting for transfers between devices  4.83 us (3%)
  loops' own time  4.23 us (2%)
    add x8, other arithmetic, one_group(): accumulated = accumulated + jnp.where(keep, shifted * weights, 0.0)  98.5 us
    dynamic_slice x16, local copies, waits for them, and re-layouts, one_group(): weights = lax.dynamic_slice_in_dim(tap_table, lag_index, 1, 0)  23.7 us
    ppermute x1, starting transfers between devices, from_behind(): return lax.ppermute(block, axis, route)  4.9 us
    all_to_all x1, starting transfers between devices, body(): lax.all_to_all(jnp.stack([catalogue] * lax.axis_size(('row', 'col'))), ax...  4.9 us
    dot_general x1, matrix products, feed_forward(): jnp.dot(columns, lax.all_gather(down_rows, 'col', axis=0, tiled=True), pr...  4.88 us
    another operation x1, loops' own time, convolve(): return lax.fori_loop(0, groups, one_group, blank)  4.23 us
    dot_general x1, matrix products, feed_forward(): jnp.dot(columns, lax.all_gather(gate_rows, 'col', axis=0, tiled=True), pr...  3.91 us
  transfers between devices with their start and end apart: 5, of which 1 were waited for; matrix products, arithmetic and copies ran while one was open for 78% of the time, Pallas kernels for 0%

profile of v1, /device:TPU:0, one launch (start us, length us, event | category | flops | bytes accessed | tf_op | source)
XLA Modules:
  0.0 174.7 jit_solution(3194262761606815539)
XLA Ops:
  8.0 4.9 %collective-permute-start = (s32[256]{0:T(256)}, s32[256]{0:T(256)S(1)}, u32[]{:S(2)}, u32[]{:S(2)}) collective-permute-start(s32[256]{0:T(256)} %param.11), channel_id=1, source_target_pairs={{0,1},{1,2},{2,3},{3,4},{4,5},{5,6},{6,7},{7,8},{8,9},{9,10},{10,1... | collective-permute-start | bytes 3080 | tf_op jit(solution)/shard_map/ppermute | solution.py:13
  12.9 1.4 stack.2
  14.3 4.9 %all-to-all-start = ((bf16[32,2,1024]{2,1,0:T(2,128)(2,1)}), bf16[32,2,1024]{2,1,0:T(2,128)(2,1)S(1)}, u32[]{:S(2)}, u32[]{:S(2)}) async-start(bf16[32,2,1024]{2,1,0:T(2,128)(2,1)} %stack.2), calls=%async_computation | async-start | bytes 262144 | tf_op jit(solution)/shard_map/all_to_all | solution.py:91
  22.3 2.2 %select_bitcast_fusion = f32[256,1024]{1,0:T(8,128)} fusion(bf16[1,256,1024]{2,1,0:T(8,128)(2,1)} %param.15, s32[1024]{0:T(1024)} %bitcast.161), kind=kLoop, calls=%fused_computation.106 | loop fusion | flops 786432 | bytes 1576960 | tf_op jit(solution)/shard_map/squeeze | solution.py:113
  24.9 2.7 %all-to-all-done = bf16[32,2,1024]{2,1,0:T(2,128)(2,1)S(1)} async-done(((bf16[32,2,1024]{2,1,0:T(2,128)(2,1)}), bf16[32,2,1024]{2,1,0:T(2,128)(2,1)S(1)}, u32[]{:S(2)}, u32[]{:S(2)}) %all-to-all-start) | async-done | bytes 131104 | tf_op jit(solution)/shard_map/all_to_all | solution.py:91
  27.6 2.1 %gather_fusion = bf16[511,1024]{1,0:T(8,128)(2,1)S(1)} fusion(bf16[64,1024]{1,0:T(8,128)(2,1)S(1)} %reshape.380, s32[1024]{0:T(1024)S(1)} %pad_clamp_fusion), kind=kCustom, calls=%fused_computation | custom fusion | bytes 2095100 | tf_op jit(solution)/shard_map/jit(_take)/gather | solution.py:108
  30.6 126.9 %while.17 = (s32[]{:T(128)}, f32[256,1024]{1,0:T(8,128)S(1)}, s32[256]{0:T(256)S(1)}, bf16[511,1024]{1,0:T(8,128)(2,1)S(1)}, f32[256,1024]{1,0:T(8,128)}, /*inde...) while((s32[]{:T(128)}, f32[256,1024]{1,0:T(8,128)S(1)}, ...), condition=%wide.region_4.5_spmd.clone, body=%wide.region_3.4_spmd.clone.sunk | while | flops 33825024 | bytes 19289948 | solution.py:50
  30.7 1.5 constant_dynamic-slice_fusion.35
  32.3 1.6 constant_dynamic-slice_fusion.34
  34.2 12.3 %select_add_fusion.3 = f32[256,1024]{1,0:T(8,128)S(1)} fusion(f32[256,1024]{1,0:T(8,128)S(1)} %get-tuple-element.605, f32[1024]{0:T(1024)S(1)} %bitcast.127, bf16[511,1024]{1,0:T(8,128)(2,1)S(1)} %get-tuple-element.679, s32[]{:T(128)S(6)} %select_n.1373, f32[1024]{0:T(1024)S(1)} %bitcast.128, s32[]{:T(128)S(6)} %select_n.1374, ...), kind=kLoop, calls=%fused_computation.26.clone.1 | loop fusion | flops 33816576 | bytes 19013760 | tf_op jit(solution)/shard_map/while/body/eval_jaxpr/add | solution.py:46
  46.7 1.4 constant_dynamic-slice_fusion.35
  48.2 1.6 constant_dynamic-slice_fusion.34
  50.2 12.3 %select_add_fusion.3 = f32[256,1024]{1,0:T(8,128)S(1)} fusion(f32[256,1024]{1,0:T(8,128)S(1)} %get-tuple-element.605, f32[1024]{0:T(1024)S(1)} %bitcast.127, bf16[511,1024]{1,0:T(8,128)(2,1)S(1)} %get-tuple-element.679, s32[]{:T(128)S(6)} %select_n.1373, f32[1024]{0:T(1024)S(1)} %bitcast.128, s32[]{:T(128)S(6)} %select_n.1374, ...), kind=kLoop, calls=%fused_computation.26.clone.1 | loop fusion | flops 33816576 | bytes 19013760 | tf_op jit(solution)/shard_map/while/body/eval_jaxpr/add | solution.py:46
  62.6 1.4 constant_dynamic-slice_fusion.35
  64.2 1.4 constant_dynamic-slice_fusion.34
  66.0 12.3 %select_add_fusion.3 = f32[256,1024]{1,0:T(8,128)S(1)} fusion(f32[256,1024]{1,0:T(8,128)S(1)} %get-tuple-element.605, f32[1024]{0:T(1024)S(1)} %bitcast.127, bf16[511,1024]{1,0:T(8,128)(2,1)S(1)} %get-tuple-element.679, s32[]{:T(128)S(6)} %select_n.1373, f32[1024]{0:T(1024)S(1)} %bitcast.128, s32[]{:T(128)S(6)} %select_n.1374, ...), kind=kLoop, calls=%fused_computation.26.clone.1 | loop fusion | flops 33816576 | bytes 19013760 | tf_op jit(solution)/shard_map/while/body/eval_jaxpr/add | solution.py:46
  78.4 1.5 constant_dynamic-slice_fusion.35
  80.0 1.7 constant_dynamic-slice_fusion.34
  82.1 12.3 %select_add_fusion.3 = f32[256,1024]{1,0:T(8,128)S(1)} fusion(f32[256,1024]{1,0:T(8,128)S(1)} %get-tuple-element.605, f32[1024]{0:T(1024)S(1)} %bitcast.127, bf16[511,1024]{1,0:T(8,128)(2,1)S(1)} %get-tuple-element.679, s32[]{:T(128)S(6)} %select_n.1373, f32[1024]{0:T(1024)S(1)} %bitcast.128, s32[]{:T(128)S(6)} %select_n.1374, ...), kind=kLoop, calls=%fused_computation.26.clone.1 | loop fusion | flops 33816576 | bytes 19013760 | tf_op jit(solution)/shard_map/while/body/eval_jaxpr/add | solution.py:46
  95.9 1.6 constant_dynamic-slice_fusion.34
  97.8 12.3 %select_add_fusion.3 = f32[256,1024]{1,0:T(8,128)S(1)} fusion(f32[256,1024]{1,0:T(8,128)S(1)} %get-tuple-element.605, f32[1024]{0:T(1024)S(1)} %bitcast.127, bf16[511,1024]{1,0:T(8,128)(2,1)S(1)} %get-tuple-element.679, s32[]{:T(128)S(6)} %select_n.1373, f32[1024]{0:T(1024)S(1)} %bitcast.128, s32[]{:T(128)S(6)} %select_n.1374, ...), kind=kLoop, calls=%fused_computation.26.clone.1 | loop fusion | flops 33816576 | bytes 19013760 | tf_op jit(solution)/shard_map/while/body/eval_jaxpr/add | solution.py:46
  111.7 1.7 constant_dynamic-slice_fusion.34
  113.7 12.3 %select_add_fusion.3 = f32[256,1024]{1,0:T(8,128)S(1)} fusion(f32[256,1024]{1,0:T(8,128)S(1)} %get-tuple-element.605, f32[1024]{0:T(1024)S(1)} %bitcast.127, bf16[511,1024]{1,0:T(8,128)(2,1)S(1)} %get-tuple-element.679, s32[]{:T(128)S(6)} %select_n.1373, f32[1024]{0:T(1024)S(1)} %bitcast.128, s32[]{:T(128)S(6)} %select_n.1374, ...), kind=kLoop, calls=%fused_computation.26.clone.1 | loop fusion | flops 33816576 | bytes 19013760 | tf_op jit(solution)/shard_map/while/body/eval_jaxpr/add | solution.py:46
  126.1 1.3 constant_dynamic-slice_fusion.35
  127.5 1.4 constant_dynamic-slice_fusion.34
  129.3 12.3 %select_add_fusion.3 = f32[256,1024]{1,0:T(8,128)S(1)} fusion(f32[256,1024]{1,0:T(8,128)S(1)} %get-tuple-element.605, f32[1024]{0:T(1024)S(1)} %bitcast.127, bf16[511,1024]{1,0:T(8,128)(2,1)S(1)} %get-tuple-element.679, s32[]{:T(128)S(6)} %select_n.1373, f32[1024]{0:T(1024)S(1)} %bitcast.128, s32[]{:T(128)S(6)} %select_n.1374, ...), kind=kLoop, calls=%fused_computation.26.clone.1 | loop fusion | flops 33816576 | bytes 19013760 | tf_op jit(solution)/shard_map/while/body/eval_jaxpr/add | solution.py:46
  141.7 1.3 constant_dynamic-slice_fusion.35
  143.2 1.6 constant_dynamic-slice_fusion.34
  145.2 12.3 %select_add_fusion.3 = f32[256,1024]{1,0:T(8,128)S(1)} fusion(f32[256,1024]{1,0:T(8,128)S(1)} %get-tuple-element.605, f32[1024]{0:T(1024)S(1)} %bitcast.127, bf16[511,1024]{1,0:T(8,128)(2,1)S(1)} %get-tuple-element.679, s32[]{:T(128)S(6)} %select_n.1373, f32[1024]{0:T(1024)S(1)} %bitcast.128, s32[]{:T(128)S(6)} %select_n.1374, ...), kind=kLoop, calls=%fused_computation.26.clone.1 | loop fusion | flops 33816576 | bytes 19013760 | tf_op jit(solution)/shard_map/while/body/eval_jaxpr/add | solution.py:46
  157.7 1.3 copy-done
  159.4 3.9 %fusion.28 = f32[256,1024]{1,0:T(8,128)} fusion(bf16[1,1024,1024]{2,1,0:T(8,128)(2,1)} %all-gather.7.cloned.1.call-done, f32[1024]{0:T(1024)S(1)} %bitcast.163, f32[256]{0:T(256)S(1)} %add_rsqrt_fusion.1, f32[256,1024]{1,0:T(8,128)S(1)} %get-tuple-element.276, f32[511,1024]{1,0:T(8,128)} %copy-done), kind=kOutput, calls=%fused_computation.95 | convolution fusion | flops 537919488 | bytes 5248000 | tf_op jit(solution)/shard_map/dot_general | solution.py:56
  163.3 4.9 %fusion.36 = bf16[256,1024]{1,0:T(8,128)(2,1)} fusion(bf16[1,1024,1024]{2,1,0:T(8,128)(2,1)} %all-gather.11.cloned.1.call-done, bf16[1,1024,1024]{2,1,0:T(8,128)(2,1)} %all-gather.9.cloned.1.call-done, f32[256,1024]{1,0:T(8,128)} %fusion.28, f32[1024]{0:T(1024)S(1)} %bitcast.164, f32[256]{0:T(256)S(1)} %add_rsqrt_fusion.1, ...), kind=kOutput, calls=%fused_computation.101 | convolution fusion | flops 1077149696 | bytes 9966592 | tf_op jit(solution)/shard_map/dot_general | solution.py:68
  (52 shorter events, 9.4 us)
Async XLA Ops:
  6.5 18.2 %copy-start.2 = (s32[256]{0:T(256)S(1)}, s32[256]{0:T(256)}, u32[]{:S(2)}) copy-start(s32[256]{0:T(256)} %param.11) | copy-start | bytes 3076
  6.5 152.8 %all-gather.7.cloned.1.call-start = ((), (), s32[]{:S(2)}) async-start(), calls=%async_computation.1 | async-start | bytes 2359296 | tf_op jit(solution)/shard_map/all_gather | solution.py:58
  7.3 156.0 %all-gather.11.cloned.1.call-start = ((), (), s32[]{:S(2)}) async-start(), calls=%async_computation.3 | async-start | bytes 2359296 | tf_op jit(solution)/shard_map/all_gather | solution.py:70
  8.0 16.6 %collective-permute-start = (s32[256]{0:T(256)}, s32[256]{0:T(256)S(1)}, u32[]{:S(2)}, u32[]{:S(2)}) collective-permute-start(s32[256]{0:T(256)} %param.11), channel_id=1, source_target_pairs={{0,1},{1,2},{2,3},{3,4},{4,5},{5,6},{6,7},{7,8},{8,9},{9,10},{10,1... | collective-permute-start | bytes 3080 | tf_op jit(solution)/shard_map/ppermute | solution.py:13
  14.3 13.3 %all-to-all-start = ((bf16[32,2,1024]{2,1,0:T(2,128)(2,1)}), bf16[32,2,1024]{2,1,0:T(2,128)(2,1)S(1)}, u32[]{:S(2)}, u32[]{:S(2)}) async-start(bf16[32,2,1024]{2,1,0:T(2,128)(2,1)} %stack.2), calls=%async_computation | async-start | bytes 262144 | tf_op jit(solution)/shard_map/all_to_all | solution.py:91
  19.2 144.1 %all-gather.9.cloned.1.call-start = ((), (), s32[]{:S(2)}) async-start(), calls=%async_computation.2 | async-start | bytes 2359296 | tf_op jit(solution)/shard_map/all_gather | solution.py:63
  157.7 1.3 copy-start
  159.4 3.9 %copy-start.1 = (f32[511,1024]{1,0:T(8,128)S(1)}, f32[511,1024]{1,0:T(8,128)}, u32[]{:S(2)}) copy-start(f32[511,1024]{1,0:T(8,128)} %copy-done) | copy-start | bytes 6279172
Sparse Core Ops, SparseCore 0:
  9.5 53.3 all-gather.6
  65.0 47.6 all-gather.10
  114.8 47.5 all-gather.8
